TPU v7x, 256 devices: a whole 4x4x8 slice. The times are simulated.
256 devices in a mesh: dp: 8 (over x, core), seq: 32 (over z, y).
Axes of the slice: x: 4, y: 4, z: 8, core: 2. Of those that a mesh axis runs over, the one named last changes fastest.
Arguments:
- queries: bfloat16 [8, 8192, 2048], P('dp', 'seq'), may hold values from -40 to 40
- keys: bfloat16 [8, 8192, 2048], P('dp', 'seq'), may hold values from -40 to 40
- values: bfloat16 [8, 8192, 2048], P('dp', 'seq'), may hold values from -6 to 6
- key_gain: float32 [2048], replicated, may hold values from 0.25 to 1.75
- random_blocks: int32 [16, 128, 3], P(None, 'seq'), may hold values from 2 to 127, as said below
- out_grad: bfloat16 [8, 8192, 2048], P('dp', 'seq'), may hold values from -6 to 6
Outputs:
- attended: bfloat16 [8, 8192, 2048], P('dp', 'seq')
- query_grad: bfloat16 [8, 8192, 2048], P('dp', 'seq')
- key_grad: bfloat16 [8, 8192, 2048], P('dp', 'seq')
- value_grad: bfloat16 [8, 8192, 2048], P('dp', 'seq')
- gain_grad: float32 [2048], replicated
Inputs may be any that keep to these rules, and one draw needn't show every extreme that they name: `random_blocks`: for the 4 query blocks of one device, all heads and entries together, at most 9 entries name blocks held by any one device (blocks d * 4 to d * 4 + 3), and exactly 9 name the blocks of some device.
All inputs are finite; a program needn't handle non-finite values.
Results may differ from a plain program's by a relative error of at most 0.03.
The roundings to bfloat16 on the way count: a program that leaves them out, or rounds other values in their place, can miss the bound.
Values may be sent and summed in bfloat16 or wider, within the bound.
No kernel may reach another device: no remote copies, remote signals or barrier semaphores. Data moves between devices by JAX's collectives and lax.ppermute only.
A program may use at most 128 MiB of HBM per device.

v0:
```python
import math
import jax
import jax.numpy as jnp
from jax import lax
from jax.sharding import PartitionSpec as P

HEADS = 16
HD = 128
BLOCK = 64
NG = 2
NR = 3
NK = 8
NEGATIVE = -1e30


def broadcast(block, axis, owner):
    block = jnp.where(lax.axis_index(axis) == owner, block, jnp.zeros_like(block))
    return lax.psum(block, axis)


def padded_2(cells, sides, width):
    for axis, dim in sides:
        count = lax.axis_size(axis)
        ends = count - 1
        head = lax.slice_in_dim(cells, 0, width, axis=dim)
        tail = lax.slice_in_dim(cells, cells.shape[dim] - width, cells.shape[dim], axis=dim)
        cells = jnp.concatenate(
            [
                lax.ppermute(tail, axis, [(i, (i + 1) % count) for i in range(ends)]),
                cells,
                lax.ppermute(head, axis, [((i + 1) % count, i) for i in range(ends)]),
            ],
            axis=dim,
        )
    return cells


def passed_along(array, axis, by):
    length = lax.axis_size(axis)
    pairs = [(i, i + by) for i in range(length) if 0 <= i + by < length]
    return lax.ppermute(array, axis, pairs)


def to_heads(rows_in):
    return rows_in.reshape(rows_in.shape[0] // BLOCK, BLOCK, HEADS, HD).transpose(2, 0, 1, 3)


def from_heads(blocks_in):
    return blocks_in.transpose(1, 2, 0, 3).reshape(1, blocks_in.shape[1] * BLOCK, HEADS * HD)


def build_list(edge_part, window_part, random_in):
    head_count = random_in.shape[0]
    block_count = random_in.shape[1]
    global_list = jnp.broadcast_to(
        edge_part[:, None], (head_count, block_count) + edge_part.shape[1:]
    )
    window_list = jnp.stack(
        [window_part[:, offset : offset + block_count] for offset in range(3)], axis=2
    )
    joined = jnp.concatenate([global_list, window_list, random_in], axis=2)
    return joined.reshape(head_count, block_count, NK * BLOCK, HD)


def spread_terms(coef, rows_in):
    head_count = rows_in.shape[0]
    block_count = rows_in.shape[1]
    coef_blocks = coef.reshape(head_count, block_count, BLOCK, NK, BLOCK)
    global_term = jnp.einsum(
        "hpbgc,hpbd->hgcd", coef_blocks[:, :, :, :NG], rows_in, preferred_element_type=jnp.float32
    )
    padded = jnp.zeros((head_count, block_count + 2, BLOCK, HD), jnp.float32)
    for offset in range(3):
        term = jnp.einsum(
            "hpbc,hpbd->hpcd",
            coef_blocks[:, :, :, NG + offset],
            rows_in,
            preferred_element_type=jnp.float32,
        )
        padded = padded + jnp.pad(term, ((0, 0), (offset, 2 - offset), (0, 0), (0, 0)))
    random_term = jnp.einsum(
        "hpbrc,hpbd->hprcd",
        coef_blocks[:, :, :, NG + 3 :],
        rows_in,
        preferred_element_type=jnp.float32,
    )
    return (global_term, padded, random_term)


def sparse_group(
    query_blk,
    edge_key,
    edge_value,
    window_key,
    window_value,
    random_key,
    random_value,
    grad_blk,
    valid_keys,
    keep_rows,
):
    score_scale = HD ** (-0.5)
    key_list = build_list(edge_key, window_key, random_key)
    value_list = build_list(edge_value, window_value, random_value)
    key_mask = jnp.repeat(valid_keys, BLOCK, axis=1)[None, :, None, :]
    scores = (
        jnp.einsum("hpbd,hpnd->hpbn", query_blk, key_list, preferred_element_type=jnp.float32)
        * score_scale
    )
    scores = jnp.where(key_mask, scores, NEGATIVE)
    row_top = jnp.max(scores, axis=3, keepdims=True)
    expo_vals = jnp.where(key_mask, jnp.exp(scores - row_top), 0.0)
    row_total = jnp.sum(expo_vals, axis=3, keepdims=True)
    numerator = jnp.einsum(
        "hpbn,hpnd->hpbd",
        expo_vals.astype(jnp.bfloat16),
        value_list,
        preferred_element_type=jnp.float32,
    )
    attended = (numerator / row_total).astype(jnp.bfloat16)
    row_delta = jnp.sum(grad_blk.astype(jnp.float32) * attended.astype(jnp.float32), axis=3)
    weights = expo_vals / row_total * keep_rows[None, :, None, None]
    dprobs = jnp.einsum("hpbd,hpnd->hpbn", grad_blk, value_list, preferred_element_type=jnp.float32)
    dscores = (weights * (dprobs - row_delta[:, :, :, None]) * score_scale).astype(jnp.bfloat16)
    dquery = jnp.einsum("hpbn,hpnd->hpbd", dscores, key_list, preferred_element_type=jnp.float32)
    key_global, key_padded, key_random = spread_terms(dscores, query_blk)
    value_global, value_padded, value_random = spread_terms(weights.astype(jnp.bfloat16), grad_blk)
    global_part = jnp.stack([key_global, value_global], axis=1)
    padded = jnp.stack([key_padded, value_padded], axis=1)
    random_part = jnp.stack([key_random, value_random], axis=1)
    return (attended, dquery, global_part, padded, random_part)


def shards(queries, keys, values, key_gain, random_blocks, out_grad):
    score_scale = HD ** (-0.5)
    tok_count = queries.shape[1]
    per_dev = tok_count // BLOCK
    owners = lax.axis_size("seq")
    seq_place = lax.axis_index("seq")
    total_blocks = owners * per_dev
    first_block = seq_place * per_dev
    key_eff = (keys[0].astype(jnp.float32) * key_gain).astype(jnp.bfloat16)
    edge_count = NG * BLOCK
    edge_rows = broadcast(
        jnp.stack(
            [
                queries[0, :edge_count],
                key_eff[:edge_count],
                values[0, :edge_count],
                out_grad[0, :edge_count],
            ]
        ),
        "seq",
        0,
    )
    window_rows = padded_2(jnp.stack([key_eff, values[0]]), (("seq", 1),), BLOCK)
    query_h = to_heads(queries[0])
    key_h = to_heads(key_eff)
    value_h = to_heads(values[0])
    grad_h = to_heads(out_grad[0])
    edge_heads = [to_heads(edge_rows[slot_pick]) for slot_pick in range(4)]
    window_key = to_heads(window_rows[0])
    window_value = to_heads(window_rows[1])
    request_count = HEADS * per_dev * NR
    capacity = (request_count + owners - 1) // owners + 3
    target = random_blocks.reshape(request_count)
    owner_dev = target // per_dev
    table_index = (
        jnp.arange(request_count, dtype=jnp.int32) // (per_dev * NR) * per_dev + target % per_dev
    )
    onehot = (owner_dev[:, None] == jnp.arange(owners, dtype=jnp.int32)[None, :]).astype(jnp.int32)
    before = jnp.cumsum(onehot, axis=0) - onehot
    slot_rank = jnp.sum(before * onehot, axis=1)
    position = owner_dev * capacity + slot_rank
    outgoing = (
        jnp.full((owners * capacity,), -1, jnp.int32)
        .at[position]
        .set(table_index)
        .reshape(owners, capacity)
    )
    kv_table = jnp.concatenate([key_h, value_h], axis=3).reshape(HEADS * per_dev, BLOCK, 2 * HD)
    index_part = lax.all_to_all(outgoing, "seq", split_axis=0, concat_axis=0, tiled=True)
    picked = kv_table[jnp.clip(index_part, 0, HEADS * per_dev - 1)]
    fetch_result = (
        lax.all_to_all(picked, "seq", split_axis=0, concat_axis=0, tiled=True),
        index_part,
    )
    arrived, served = fetch_result
    fetched = arrived.reshape(owners * capacity, BLOCK, 2 * HD)[position].reshape(
        HEADS, per_dev, NR, BLOCK, 2 * HD
    )
    fetched_key = fetched[..., :HD]
    fetched_value = fetched[..., HD:]
    block_index = first_block + jnp.arange(per_dev, dtype=jnp.int32)
    window_index = block_index[:, None] + jnp.arange(-1, 2, dtype=jnp.int32)[None, :]
    valid_keys = jnp.concatenate(
        [
            jnp.ones((per_dev, NG), bool),
            (window_index >= NG) & (window_index < total_blocks),
            jnp.ones((per_dev, NR), bool),
        ],
        axis=1,
    )
    keep_rows = (block_index >= NG).astype(jnp.float32)
    group_size = math.gcd(HEADS, 4)

    def by_group(array_in):
        return array_in.reshape((HEADS // group_size, group_size) + array_in.shape[1:])

    def merge_groups(array_in):
        return array_in.reshape((HEADS,) + array_in.shape[2:])

    def run_group(bundle):
        return sparse_group(
            bundle[0],
            bundle[1],
            bundle[2],
            bundle[3],
            bundle[4],
            bundle[5],
            bundle[6],
            bundle[7],
            valid_keys,
            keep_rows,
        )

    grouped = lax.map(
        run_group,
        (
            by_group(query_h),
            by_group(edge_heads[1]),
            by_group(edge_heads[2]),
            by_group(window_key),
            by_group(window_value),
            by_group(fetched_key),
            by_group(fetched_value),
            by_group(grad_h),
        ),
    )
    attended_h, dquery_h, global_part, padded, random_part = [
        merge_groups(piece_out) for piece_out in grouped
    ]
    edge_query = edge_heads[0].reshape(HEADS, edge_count, HD)
    edge_grad = edge_heads[3].reshape(HEADS, edge_count, HD)
    flat_key = key_h.reshape(HEADS, tok_count, HD)
    flat_value = value_h.reshape(HEADS, tok_count, HD)
    edge_scores = (
        jnp.einsum("hqd,htd->hqt", edge_query, flat_key, preferred_element_type=jnp.float32)
        * score_scale
    )
    edge_top = lax.pmax(jnp.max(edge_scores, axis=2), "seq")
    edge_expo = jnp.exp(edge_scores - edge_top[:, :, None])
    edge_total, edge_numer = lax.psum(
        (
            jnp.sum(edge_expo, axis=2),
            jnp.einsum(
                "hqt,htd->hqd",
                edge_expo.astype(jnp.bfloat16),
                flat_value,
                preferred_element_type=jnp.float32,
            ),
        ),
        "seq",
    )
    edge_out = (edge_numer / edge_total[:, :, None]).astype(jnp.bfloat16)
    edge_delta = jnp.sum(edge_grad.astype(jnp.float32) * edge_out.astype(jnp.float32), axis=2)
    edge_weights = edge_expo / edge_total[:, :, None]
    edge_dprobs = jnp.einsum(
        "hqd,htd->hqt", edge_grad, flat_value, preferred_element_type=jnp.float32
    )
    edge_dscores = (edge_weights * (edge_dprobs - edge_delta[:, :, None]) * score_scale).astype(
        jnp.bfloat16
    )
    edge_dquery = jnp.einsum(
        "hqt,htd->hqd", edge_dscores, flat_key, preferred_element_type=jnp.float32
    )
    local_dkey = jnp.einsum(
        "hqt,hqd->htd", edge_dscores, edge_query, preferred_element_type=jnp.float32
    )
    local_dvalue = jnp.einsum(
        "hqt,hqd->htd",
        edge_weights.astype(jnp.bfloat16),
        edge_grad,
        preferred_element_type=jnp.float32,
    )
    random_rounded = (
        random_part.transpose(0, 2, 3, 4, 1, 5)
        .reshape(request_count, BLOCK, 2 * HD)
        .astype(jnp.bfloat16)
    )
    sendback = (
        jnp.zeros((owners * capacity, BLOCK, 2 * HD), jnp.bfloat16)
        .at[position]
        .set(random_rounded)
        .reshape(owners, capacity, BLOCK, 2 * HD)
    )
    returned = lax.all_to_all(sendback, "seq", split_axis=0, concat_axis=0, tiled=True)
    owner_table = (
        served.reshape(1, owners * capacity)
        == jnp.arange(HEADS * per_dev, dtype=jnp.int32)[:, None]
    ).astype(jnp.bfloat16)
    summed = jnp.dot(
        owner_table,
        returned.reshape(owners * capacity, BLOCK * 2 * HD),
        preferred_element_type=jnp.float32,
    )
    summed = summed.reshape(HEADS, per_dev, BLOCK, 2, HD).transpose(0, 3, 1, 2, 4)
    from_right = passed_along(padded[:, :, 0].astype(jnp.bfloat16), "seq", -1).astype(jnp.float32)
    from_left = passed_along(padded[:, :, per_dev + 1].astype(jnp.bfloat16), "seq", 1).astype(
        jnp.float32
    )
    edge_dquery_sum, global_sum = lax.psum((edge_dquery, global_part), "seq")
    accum = padded[:, :, 1 : per_dev + 1]
    accum = accum + jnp.stack([local_dkey, local_dvalue], axis=1).reshape(
        HEADS, 2, per_dev, BLOCK, HD
    )
    accum = accum + summed
    accum = accum.at[:, :, per_dev - 1].add(from_right)
    accum = accum.at[:, :, 0].add(from_left)
    is_first = (seq_place == 0).astype(jnp.float32)
    accum = accum.at[:, :, :NG].add(global_sum * is_first)
    is_edge = (block_index < NG)[None, :, None, None]
    tail_zeros = jnp.zeros((HEADS, per_dev - NG, BLOCK, HD), jnp.float32)
    edge_dq_blocks = jnp.concatenate(
        [edge_dquery_sum.reshape(HEADS, NG, BLOCK, HD), tail_zeros], axis=1
    )
    edge_out_blocks = jnp.concatenate(
        [edge_out.reshape(HEADS, NG, BLOCK, HD), tail_zeros.astype(jnp.bfloat16)], axis=1
    )
    dquery_all = jnp.where(is_edge, edge_dq_blocks, dquery_h).astype(jnp.bfloat16)
    attended_all = jnp.where(is_edge, edge_out_blocks, attended_h)
    key_eff_grad = accum[:, 0]
    gain_heads = key_gain.reshape(HEADS, HD)
    key_grad_h = (key_eff_grad * gain_heads[:, None, None, :]).astype(jnp.bfloat16)
    value_grad_h = accum[:, 1].astype(jnp.bfloat16)
    gain_term = jnp.sum(key_eff_grad * to_heads(keys[0]).astype(jnp.float32), axis=(1, 2)).reshape(
        HEADS * HD
    )
    gain_grad = lax.psum(gain_term, ("dp", "seq"))
    return (
        from_heads(attended_all),
        from_heads(dquery_all),
        from_heads(key_grad_h),
        from_heads(value_grad_h),
        gain_grad,
    )


def solution(mesh):
    placed = (
        P("dp", "seq", None),
        P("dp", "seq", None),
        P("dp", "seq", None),
        P(),
        P(None, "seq", None),
        P("dp", "seq", None),
    )
    return jax.shard_map(
        shards,
        mesh=mesh,
        in_specs=placed,
        out_specs=(
            P("dp", "seq", None),
            P("dp", "seq", None),
            P("dp", "seq", None),
            P("dp", "seq", None),
            P(),
        ),
        check_vma=False,
    )
```

profile of v0, /device:TPU:1, one launch (start us, length us, event | category | flops | bytes accessed | tf_op | source)
XLA Modules:
  0.0 1441.6 jit_solution(389370633972243564)
XLA Ops:
  11.2 12.0 all-to-all-start
  33.7 10.3 gather_fusion
  43.9 7.5 all-to-all-start.1
  58.0 3.9 collective-permute-start
  68.2 25.1 %collective-permute-done = bf16[2,64,2048]{2,1,0:T(8,128)(2,1)} collective-permute-done((bf16[2,64,2048]{2,1,0:T(8,128)(2,1)}, bf16[2,64,2048]{2,1,0:T(8,128)(2,1)}, u32[]{:S(2)}, u32[]{:S(2)}) %collective-permute-start) | collective-permute-done | bytes 524320 | tf_op jit(solution)/shard_map/ppermute | solution.py:29
  93.3 21.3 %collective-permute-done.1 = bf16[2,64,2048]{2,1,0:T(8,128)(2,1)} collective-permute-done((bf16[2,64,2048]{2,1,0:T(8,128)(2,1)}, bf16[2,64,2048]{2,1,0:T(8,128)(2,1)}, u32[]{:S(2)}, u32[]{:S(2)}) %collective-permute-start.1) | collective-permute-done | bytes 524320 | tf_op jit(solution)/shard_map/ppermute | solution.py:31
  119.1 206.0 %all-reduce.14.cloned.1.call-done = bf16[4,128,2048]{2,1,0:T(8,128)(2,1)} async-done(((bf16[4,128,2048]{2,1,0:T(8,128)(2,1)}), bf16[4,128,2048]{2,1,0:T(8,128)(2,1)}) %all-reduce.14.cloned.1.call-update) | async-done | bytes 2097168 | tf_op jit(solution)/shard_map/psum | solution.py:18
  329.1 11.8 gather_fusion.1
  340.9 8.0 fusion.134
  348.9 287.8 %while.24 = (s32[]{:T(128)}, bf16[4,4,4,64,128]{4,3,2,1,0:T(8,128)(2,1)}, bf16[4,4,4,64,128]{4,3,2,1,0:T(8,128)(2,1)}, f32[4,4,2,2,64,128]{5,1,0,2,4,3:T(4,128)}...) while((s32[]{:T(128)}, ...), condition=%wide.region_14.15_spmd.clone, body=%wide.region_10.14_spmd.clone.sunk | while | flops 952370176 | bytes 142396560 | solution.py:227
  356.1 3.5 fusion.232
  368.6 5.1 bitcast_dynamic-update-slice_fusion.6
  427.9 3.5 fusion.232
  440.4 5.1 bitcast_dynamic-update-slice_fusion.6
  499.7 3.5 fusion.232
  512.2 5.1 bitcast_dynamic-update-slice_fusion.6
  571.5 3.5 fusion.232
  584.1 5.1 bitcast_dynamic-update-slice_fusion.6
  636.7 12.7 copy.168
  649.4 10.8 reshape.529
  660.3 4.9 broadcast_in_dim.167
  665.1 29.1 %scatter_fusion = bf16[288,64,256]{2,1,0:T(8,128)(2,1)} fusion(bf16[288,64,256]{2,1,0:T(8,128)(2,1)} %broadcast_in_dim.167, s32[192]{0:T(256)S(1)} %bitcast.511, bf16[192,64,256]{2,1,0:T(8,128)(2,1)} %reshape.529), kind=kCustom, calls=%fused_computation.3 | custom fusion | bytes 18875136 | tf_op jit(solution)/shard_map/scatter | solution.py:294
  694.3 6.0 all-to-all-start.2
  704.3 248.7 %pmax.7 = f32[16,128]{1,0:T(8,128)S(1)} all-reduce(f32[16,128]{1,0:T(8,128)S(1)} %get-tuple-element.352), channel_id=1, replica_groups=mesh['dp'=8,'seq'=32] {'seq'}, use_global_device_ids=true, to_apply=%region_2.3 | all-reduce | flops 2048 | bytes 16384 | tf_op jit(solution)/shard_map/pmax | solution.py:251
  960.4 59.2 %psum.44 = f32[16,128]{1,0:T(8,128)S(1)} all-reduce(f32[16,128]{1,0:T(8,128)S(1)} %fusion.95), channel_id=1, replica_groups=mesh['dp'=8,'seq'=32] {'seq'}, use_global_device_ids=true, to_apply=%region_5.6 | all-reduce | flops 2048 | bytes 16384 | tf_op jit(solution)/shard_map/psum | solution.py:253
  1028.2 4.8 collective-permute-start.3
  1033.0 99.2 %all-reduce.16.cloned.1.call-done = (f32[16,128,128]{2,1,0:T(8,128)}, f32[16,2,2,64,128]{4,0,1,3,2:T(8,128)}) async-done(((f32[16,128,128]{2,1,0:T(8,128)}, f32[16,2,2,64,128]{4,0,1,3,2:T(8,128)}), (f32[16,128,128]{2,1,0:T(8,128)}, f32[16,2,2,64,128]{4,0,1,3,2:T(8,128)})) %all-reduce.16.cloned.1.call-update) | async-done | bytes 3145744 | tf_op jit(solution)/shard_map/psum | solution.py:253
  1141.9 123.4 %all-reduce.17 = bf16[16,2,64,128]{3,2,1,0:T(8,128)(2,1)S(1)} all-reduce(f32[16,2,64,128]{3,2,1,0:T(8,128)} %bitcast.485), channel_id=1, replica_groups=mesh['dp'=8,'seq'=32] {'seq'}, use_global_device_ids=true, to_apply=%region_16.17 | all-reduce | flops 262144 | bytes 1572864 | tf_op jit(solution)/shard_map/psum | solution.py:312
  1273.5 18.5 %copy.212 = bf16[36,8,64,256]{3,1,2,0:T(8,128)(2,1)} copy(bf16[36,8,64,256]{3,2,1,0:T(8,128)(2,1)} %bitcast.182) | data formatting | bytes 18874368
  1292.0 16.1 %dot_general.116 = bf16[64,2,128,288]{2,1,0,3:T(2,128)(2,1)} reshape(bf16[16384,288]{0,1:T(8,128)(2,1)} %bitcast.460) | data formatting | bytes 18874368 | tf_op jit(solution)/shard_map/dot_general | solution.py:302
  1308.1 12.3 fusion.85
  1328.3 106.2 %psum.47 = f32[2048]{0:T(1024)} all-reduce(f32[2048]{0:T(1024)S(1)} %bitcast.508), channel_id=1, replica_groups=mesh['dp'=8,'seq'=32] {'dp','seq'}, use_global_device_ids=true, to_apply=%region_20.21 | all-reduce | flops 2048 | bytes 16384 | tf_op jit(solution)/shard_map/psum | solution.py:339
  (469 shorter events, 332.3 us)
Async XLA Ops:
  9.3 58.8 %copy-start.31 = (s32[192,1]{0,1:T(1,128)}, s32[192,1]{0,1:T(1,128)S(1)}, u32[]{:S(2)}) copy-start(s32[192,1]{0,1:T(1,128)S(1)} %compare_select_fusion.1) | copy-start | bytes 2308
  11.2 20.6 %all-to-all-start = ((s32[32,1,9]{2,1,0:T(1,128)}), s32[32,1,9]{2,1,0:T(1,128)S(1)}, u32[]{:S(2)}, u32[]{:S(2)}) async-start(s32[32,1,9]{2,1,0:T(1,128)} %bitcast.20), calls=%async_computation | async-start | bytes 32768 | tf_op jit(solution)/shard_map/all_to_all | solution.py:182
  43.9 285.2 %all-to-all-start.1 = ((bf16[32,9,64,256]{3,2,1,0:T(8,128)(2,1)}), bf16[32,9,64,256]{3,2,1,0:T(8,128)(2,1)}, u32[]{:S(2)}, u32[]{:S(2)}) async-start(bf16[32,9,64,256]{3,2,1,0:T(8,128)(2,1)} %bitcast.459), calls=%async_computation.1 | async-start | bytes 18874368 | tf_op jit(solution)/shard_map/all_to_all | solution.py:185
  51.4 273.7 %all-reduce.14.cloned.1.call-start = ((), (), s32[]{:S(2)}) async-start(), calls=%async_computation.3 | async-start | bytes 4194304 | tf_op jit(solution)/shard_map/psum | solution.py:18
  58.0 35.3 %collective-permute-start = (bf16[2,64,2048]{2,1,0:T(8,128)(2,1)}, bf16[2,64,2048]{2,1,0:T(8,128)(2,1)}, u32[]{:S(2)}, u32[]{:S(2)}) collective-permute-start(bf16[2,64,2048]{2,1,0:T(8,128)(2,1)} %get-tuple-element.342), channel_id=1, source_target_pairs={{0,1},{1,2},{2,3},{3,4},{4,5},{5,6},{6,7},{7,8},{8,9},{9,10},{10,1... | collective-permute-start | bytes 1572872 | tf_op jit(solution)/shard_map/ppermute | solution.py:29
  61.8 52.8 %collective-permute-start.1 = (bf16[2,64,2048]{2,1,0:T(8,128)(2,1)}, bf16[2,64,2048]{2,1,0:T(8,128)(2,1)}, u32[]{:S(2)}, u32[]{:S(2)}) collective-permute-start(bf16[2,64,2048]{2,1,0:T(8,128)(2,1)} %get-tuple-element.343), channel_id=1, source_target_pairs={{1,0},{2,1},{3,2},{4,3},{5,4},{6,5},{7,6},{8,7},{9,8},{10,9},{11,1... | collective-permute-start | bytes 1572872 | tf_op jit(solution)/shard_map/ppermute | solution.py:31
  355.9 3.7 copy-start.1
  362.6 2.9 copy-start.2
  380.2 3.8 copy-start.5
  382.5 2.9 copy-start
  427.7 3.7 copy-start.1
  434.4 2.9 copy-start.2
  452.0 3.8 copy-start.5
  454.3 2.9 copy-start
  499.5 3.7 copy-start.1
  506.2 2.9 copy-start.2
  523.8 3.8 copy-start.5
  526.0 3.0 copy-start
  571.3 3.7 copy-start.1
  578.0 2.9 copy-start.2
  595.6 3.8 copy-start.5
  597.9 2.8 copy-start
  660.3 4.9 copy-start.32
  694.3 6.1 copy-start.7
  694.3 6.1 copy-start.29
  694.3 579.3 %all-to-all-start.2 = ((bf16[32,9,64,256]{3,2,1,0:T(8,128)(2,1)}), bf16[32,9,64,256]{3,2,1,0:T(8,128)(2,1)}, u32[]{:S(2)}, u32[]{:S(2)}) async-start(bf16[32,9,64,256]{3,2,1,0:T(8,128)(2,1)} %bitcast.457), calls=%async_computation.2 | async-start | bytes 18874368 | tf_op jit(solution)/shard_map/all_to_all | solution.py:297
  700.3 432.0 %all-reduce.16.cloned.1.call-start = ((), (), s32[]{:S(2)}) async-start(), calls=%async_computation.4 | async-start | bytes 6291456 | tf_op jit(solution)/shard_map/psum | solution.py:253
  1019.5 5.5 slice-start.1
  1019.5 5.5 slice-start.2
  1026.9 293.5 %collective-permute-start.2 = (bf16[16,2,64,128]{3,0,1,2:T(8,128)(2,1)}, bf16[16,2,64,128]{3,0,1,2:T(8,128)(2,1)}, u32[]{:S(2)}, u32[]{:S(2)}) collective-permute-start(bf16[16,2,64,128]{3,0,1,2:T(8,128)(2,1)} %get-tuple-element.335), channel_id=1, source_target_pairs={{1,0},{2,1},{3,2},{4,3},{5,4},{6,5},{7,6},{8,7},{9,8},{10,9},{11,1... | collective-permute-start | bytes 1572872 | tf_op jit(solution)/shard_map/ppermute | solution.py:41
  1028.2 293.7 %collective-permute-start.3 = (bf16[16,2,64,128]{3,0,1,2:T(8,128)(2,1)}, bf16[16,2,64,128]{3,0,1,2:T(8,128)(2,1)}, u32[]{:S(2)}, u32[]{:S(2)}) collective-permute-start(bf16[16,2,64,128]{3,0,1,2:T(8,128)(2,1)} %get-tuple-element.334), channel_id=1, source_target_pairs={{0,1},{1,2},{2,3},{3,4},{4,5},{5,6},{6,7},{7,8},{8,9},{9,10},{10,1... | collective-permute-start | bytes 1572872 | tf_op jit(solution)/shard_map/ppermute | solution.py:41
  1320.5 2.8 copy-start.23
  (57 other events, 98.0 us)
Sparse Core Ops, SparseCore 0:
  55.8 269.2 all-reduce.13
  956.7 175.5 all-reduce.15
where the time goes:
time: 1450 us; the launch traced here: 1440 us
  blocking collectives  538 us (37%)
  waiting for transfers between devices  353 us (24%)
  local copies, waits for them, and re-layouts  289 us (20%)
  matrix products  154 us (11%)
  other arithmetic  53.4 us (4%)
  starting transfers between devices  37.3 us (3%)
  between operations  14.9 us (1%)
    pmax x1, blocking collectives, shards(): edge_top = lax.pmax(jnp.max(edge_scores, axis=2), 'seq')  249 us
    psum x1, waiting for transfers between devices, broadcast(): return lax.psum(block, axis)  206 us
    psum x1, blocking collectives, shards(): edge_dquery_sum, global_sum = lax.psum((edge_dquery, global_part), 'seq')  123 us
    psum x1, blocking collectives, shards(): gain_grad = lax.psum(gain_term, ('dp', 'seq'))  106 us
    psum x1, waiting for transfers between devices, shards(): lax.psum((jnp.sum(edge_expo, axis=2), jnp.einsum('hqt,htd->hqd', edge_exp...  99.2 us
    psum x1, blocking collectives, shards(): lax.psum((jnp.sum(edge_expo, axis=2), jnp.einsum('hqt,htd->hqd', edge_exp...  59.2 us
    while x160, local copies, waits for them, and re-layouts  46.8 us
    dot_general x24, matrix products, spread_terms(): jnp.einsum('hpbc,hpbd->hpcd', coef_blocks[:, :, :, NG + offset], rows_in,...  41.4 us
  transfers between devices with their start and end apart: 9, of which 5 were waited for; matrix products, arithmetic and copies ran while one was open for 7% of the time, Pallas kernels for 0%

commit v1 on v0

--- a/solution.py
+++ b/solution.py
@@ -336,7 +336,9 @@
     gain_term = jnp.sum(key_eff_grad * to_heads(keys[0]).astype(jnp.float32), axis=(1, 2)).reshape(
         HEADS * HD
     )
-    gain_grad = lax.psum(gain_term, ("dp", "seq"))
+    gain_grad = gain_term
+    for name in ("seq", "dp"):
+        gain_grad = lax.psum(gain_grad, name)
     return (
         from_heads(attended_all),
         from_heads(dquery_all),

time: 1450 us -> 1390 us (0.959)
  blocking collectives: 538 us -> 478 us
    psum x1, blocking collectives: 106 us -> 44.1 us  [shards(): gain_grad = lax.psum(gain_grad, name)]
    unnamed x58 -> x62, local copies, waits for them, and re-layouts: 33.7 us -> 34 us
where the time goes in v1:
time: 1390 us; the launch traced here: 1380 us
  blocking collectives  478 us (34%)
  waiting for transfers between devices  350 us (25%)
  local copies, waits for them, and re-layouts  288 us (21%)
  matrix products  154 us (11%)
  other arithmetic  53.3 us (4%)
  starting transfers between devices  37.2 us (3%)
  between operations  14.9 us (1%)
    pmax x1, blocking collectives, shards(): edge_top = lax.pmax(jnp.max(edge_scores, axis=2), 'seq')  248 us
    psum x1, waiting for transfers between devices, broadcast(): return lax.psum(block, axis)  203 us
    psum x1, blocking collectives, shards(): edge_dquery_sum, global_sum = lax.psum((edge_dquery, global_part), 'seq')  126 us
    psum x1, waiting for transfers between devices, shards(): lax.psum((jnp.sum(edge_expo, axis=2), jnp.einsum('hqt,htd->hqd', edge_exp...  98.6 us
    psum x1, blocking collectives, shards(): lax.psum((jnp.sum(edge_expo, axis=2), jnp.einsum('hqt,htd->hqd', edge_exp...  58.9 us
    while x160, local copies, waits for them, and re-layouts  46.8 us
    psum x1, blocking collectives, shards(): gain_grad = lax.psum(gain_grad, name)  44.1 us
    dot_general x24, matrix products, spread_terms(): jnp.einsum('hpbc,hpbd->hpcd', coef_blocks[:, :, :, NG + offset], rows_in,...  41.3 us
  transfers between devices with their start and end apart: 9, of which 5 were waited for; matrix products, arithmetic and copies ran while one was open for 7% of the time, Pallas kernels for 0%

profile of v1, /device:TPU:1, one launch (start us, length us, event | category | flops | bytes accessed | tf_op | source)
XLA Modules:
  0.0 1376.8 jit_solution(17663348680609651590)
XLA Ops:
  11.2 12.0 all-to-all-start
  33.7 10.3 gather_fusion
  43.9 7.5 all-to-all-start.1
  57.9 3.9 collective-permute-start
  68.0 25.2 %collective-permute-done = bf16[2,64,2048]{2,1,0:T(8,128)(2,1)} collective-permute-done((bf16[2,64,2048]{2,1,0:T(8,128)(2,1)}, bf16[2,64,2048]{2,1,0:T(8,128)(2,1)}, u32[]{:S(2)}, u32[]{:S(2)}) %collective-permute-start) | collective-permute-done | bytes 524320 | tf_op jit(solution)/shard_map/ppermute | solution.py:29
  93.2 21.3 %collective-permute-done.1 = bf16[2,64,2048]{2,1,0:T(8,128)(2,1)} collective-permute-done((bf16[2,64,2048]{2,1,0:T(8,128)(2,1)}, bf16[2,64,2048]{2,1,0:T(8,128)(2,1)}, u32[]{:S(2)}, u32[]{:S(2)}) %collective-permute-start.1) | collective-permute-done | bytes 524320 | tf_op jit(solution)/shard_map/ppermute | solution.py:31
  119.1 203.4 %all-reduce.15.cloned.1.call-done = bf16[4,128,2048]{2,1,0:T(8,128)(2,1)} async-done(((bf16[4,128,2048]{2,1,0:T(8,128)(2,1)}), bf16[4,128,2048]{2,1,0:T(8,128)(2,1)}) %all-reduce.15.cloned.1.call-update) | async-done | bytes 2097168 | tf_op jit(solution)/shard_map/psum | solution.py:18
  326.4 11.8 gather_fusion.1
  338.2 8.1 fusion.134
  346.3 287.8 %while.24 = (s32[]{:T(128)}, bf16[4,4,4,64,128]{4,3,2,1,0:T(8,128)(2,1)}, bf16[4,4,4,64,128]{4,3,2,1,0:T(8,128)(2,1)}, f32[4,4,2,2,64,128]{5,1,0,2,4,3:T(4,128)}...) while((s32[]{:T(128)}, ...), condition=%wide.region_14.15_spmd.clone, body=%wide.region_10.14_spmd.clone.sunk | while | flops 952370176 | bytes 142396560 | solution.py:227
  353.8 3.5 fusion.232
  366.3 5.2 bitcast_dynamic-update-slice_fusion.6
  425.5 3.5 fusion.232
  438.1 5.2 bitcast_dynamic-update-slice_fusion.6
  497.3 3.5 fusion.232
  509.8 5.2 bitcast_dynamic-update-slice_fusion.6
  569.1 3.5 fusion.232
  581.6 5.2 bitcast_dynamic-update-slice_fusion.6
  634.1 12.7 copy.168
  646.7 10.8 reshape.529
  657.6 4.9 broadcast_in_dim.167
  662.5 28.8 %scatter_fusion = bf16[288,64,256]{2,1,0:T(8,128)(2,1)} fusion(bf16[288,64,256]{2,1,0:T(8,128)(2,1)} %broadcast_in_dim.167, s32[192]{0:T(256)S(1)} %bitcast.510, bf16[192,64,256]{2,1,0:T(8,128)(2,1)} %reshape.529), kind=kCustom, calls=%fused_computation.3 | custom fusion | bytes 18875136 | tf_op jit(solution)/shard_map/scatter | solution.py:294
  691.2 5.9 all-to-all-start.2
  701.1 248.4 %pmax.7 = f32[16,128]{1,0:T(8,128)S(1)} all-reduce(f32[16,128]{1,0:T(8,128)S(1)} %get-tuple-element.354), channel_id=1, replica_groups=mesh['dp'=8,'seq'=32] {'seq'}, use_global_device_ids=true, to_apply=%region_2.3 | all-reduce | flops 2048 | bytes 16384 | tf_op jit(solution)/shard_map/pmax | solution.py:251
  956.9 58.9 %psum.51 = f32[16,128]{1,0:T(8,128)S(1)} all-reduce(f32[16,128]{1,0:T(8,128)S(1)} %fusion.95), channel_id=1, replica_groups=mesh['dp'=8,'seq'=32] {'seq'}, use_global_device_ids=true, to_apply=%region_5.6 | all-reduce | flops 2048 | bytes 16384 | tf_op jit(solution)/shard_map/psum | solution.py:253
  1024.5 5.0 collective-permute-start.3
  1029.5 98.6 %all-reduce.17.cloned.1.call-done = (f32[16,128,128]{2,1,0:T(8,128)}, f32[16,2,2,64,128]{4,0,1,3,2:T(8,128)}) async-done(((f32[16,128,128]{2,1,0:T(8,128)}, f32[16,2,2,64,128]{4,0,1,3,2:T(8,128)}), (f32[16,128,128]{2,1,0:T(8,128)}, f32[16,2,2,64,128]{4,0,1,3,2:T(8,128)})) %all-reduce.17.cloned.1.call-update) | async-done | bytes 3145744 | tf_op jit(solution)/shard_map/psum | solution.py:253
  1137.7 18.9 %copy.212 = bf16[36,8,64,256]{3,1,2,0:T(8,128)(2,1)} copy(bf16[36,8,64,256]{3,2,1,0:T(8,128)(2,1)} %bitcast.182) | data formatting | bytes 18874368
  1156.6 16.0 %dot_general.116 = bf16[64,2,128,288]{2,1,0,3:T(2,128)(2,1)} reshape(bf16[16384,288]{0,1:T(8,128)(2,1)} %bitcast.459) | data formatting | bytes 18874368 | tf_op jit(solution)/shard_map/dot_general | solution.py:302
  1172.6 12.3 fusion.85
  1191.1 126.3 %all-reduce.18 = (bf16[16,2,64,128]{3,2,1,0:T(8,128)(2,1)S(1)}, f32[2048]{0:T(1024)S(1)}) all-reduce(f32[16,2,64,128]{3,2,1,0:T(8,128)S(1)} %bitcast.484, f32[2048]{0:T(1024)S(1)} %bitcast.507), channel_id=1, replica_groups=mesh['dp'=8,'seq'=32] {'seq'}, use_global_device_ids=true, to_apply=%region_16.17 | all-reduce | flops 264192 | bytes 1589248 | tf_op jit(solution)/shard_map/psum | solution.py:312
  1325.7 44.1 %psum.55 = f32[2048]{0:T(1024)} all-reduce(f32[2048]{0:T(1024)S(1)} %get-tuple-element.315), channel_id=1, replica_groups=mesh['dp'=8,'seq'=32] {'dp'}, use_global_device_ids=true, to_apply=%region_21.22 | all-reduce | flops 2048 | bytes 16384 | tf_op jit(solution)/shard_map/psum | solution.py:341
  (473 shorter events, 330.3 us)
Async XLA Ops:
  9.3 58.6 %copy-start.33 = (s32[192,1]{0,1:T(1,128)}, s32[192,1]{0,1:T(1,128)S(1)}, u32[]{:S(2)}) copy-start(s32[192,1]{0,1:T(1,128)S(1)} %compare_select_fusion.1) | copy-start | bytes 2308
  11.2 20.6 %all-to-all-start = ((s32[32,1,9]{2,1,0:T(1,128)}), s32[32,1,9]{2,1,0:T(1,128)S(1)}, u32[]{:S(2)}, u32[]{:S(2)}) async-start(s32[32,1,9]{2,1,0:T(1,128)} %bitcast.20), calls=%async_computation | async-start | bytes 32768 | tf_op jit(solution)/shard_map/all_to_all | solution.py:182
  43.9 282.5 %all-to-all-start.1 = ((bf16[32,9,64,256]{3,2,1,0:T(8,128)(2,1)}), bf16[32,9,64,256]{3,2,1,0:T(8,128)(2,1)}, u32[]{:S(2)}, u32[]{:S(2)}) async-start(bf16[32,9,64,256]{3,2,1,0:T(8,128)(2,1)} %bitcast.458), calls=%async_computation.1 | async-start | bytes 18874368 | tf_op jit(solution)/shard_map/all_to_all | solution.py:185
  51.4 271.0 %all-reduce.15.cloned.1.call-start = ((), (), s32[]{:S(2)}) async-start(), calls=%async_computation.3 | async-start | bytes 4194304 | tf_op jit(solution)/shard_map/psum | solution.py:18
  57.9 35.3 %collective-permute-start = (bf16[2,64,2048]{2,1,0:T(8,128)(2,1)}, bf16[2,64,2048]{2,1,0:T(8,128)(2,1)}, u32[]{:S(2)}, u32[]{:S(2)}) collective-permute-start(bf16[2,64,2048]{2,1,0:T(8,128)(2,1)} %get-tuple-element.344), channel_id=1, source_target_pairs={{0,1},{1,2},{2,3},{3,4},{4,5},{5,6},{6,7},{7,8},{8,9},{9,10},{10,1... | collective-permute-start | bytes 1572872 | tf_op jit(solution)/shard_map/ppermute | solution.py:29
  61.8 52.7 %collective-permute-start.1 = (bf16[2,64,2048]{2,1,0:T(8,128)(2,1)}, bf16[2,64,2048]{2,1,0:T(8,128)(2,1)}, u32[]{:S(2)}, u32[]{:S(2)}) collective-permute-start(bf16[2,64,2048]{2,1,0:T(8,128)(2,1)} %get-tuple-element.345), channel_id=1, source_target_pairs={{1,0},{2,1},{3,2},{4,3},{5,4},{6,5},{7,6},{8,7},{9,8},{10,9},{11,1... | collective-permute-start | bytes 1572872 | tf_op jit(solution)/shard_map/ppermute | solution.py:31
  353.6 3.7 copy-start.1
  360.3 2.9 copy-start.2
  377.9 3.8 copy-start.5
  380.2 2.9 copy-start
  425.4 3.7 copy-start.1
  432.1 2.9 copy-start.2
  449.6 3.8 copy-start.5
  451.9 2.9 copy-start
  497.1 3.7 copy-start.1
  503.8 2.9 copy-start.2
  521.4 3.8 copy-start.5
  523.6 3.0 copy-start
  568.9 3.7 copy-start.1
  575.6 2.9 copy-start.2
  593.2 3.8 copy-start.5
  595.5 2.9 copy-start
  657.6 4.9 copy-start.34
  691.2 6.0 copy-start.7
  691.2 6.0 copy-start.31
  691.2 446.5 %all-to-all-start.2 = ((bf16[32,9,64,256]{3,2,1,0:T(8,128)(2,1)}), bf16[32,9,64,256]{3,2,1,0:T(8,128)(2,1)}, u32[]{:S(2)}, u32[]{:S(2)}) async-start(bf16[32,9,64,256]{3,2,1,0:T(8,128)(2,1)} %bitcast.456), calls=%async_computation.2 | async-start | bytes 18874368 | tf_op jit(solution)/shard_map/all_to_all | solution.py:297
  697.2 430.9 %all-reduce.17.cloned.1.call-start = ((), (), s32[]{:S(2)}) async-start(), calls=%async_computation.4 | async-start | bytes 6291456 | tf_op jit(solution)/shard_map/psum | solution.py:253
  1015.8 5.5 slice-start.1
  1015.8 5.5 slice-start.2
  1023.2 161.7 %collective-permute-start.2 = (bf16[16,2,64,128]{3,0,1,2:T(8,128)(2,1)}, bf16[16,2,64,128]{3,0,1,2:T(8,128)(2,1)}, u32[]{:S(2)}, u32[]{:S(2)}) collective-permute-start(bf16[16,2,64,128]{3,0,1,2:T(8,128)(2,1)} %get-tuple-element.337), channel_id=1, source_target_pairs={{1,0},{2,1},{3,2},{4,3},{5,4},{6,5},{7,6},{8,7},{9,8},{10,9},{11,1... | collective-permute-start | bytes 1572872 | tf_op jit(solution)/shard_map/ppermute | solution.py:41
  1024.5 161.9 %collective-permute-start.3 = (bf16[16,2,64,128]{3,0,1,2:T(8,128)(2,1)}, bf16[16,2,64,128]{3,0,1,2:T(8,128)(2,1)}, u32[]{:S(2)}, u32[]{:S(2)}) collective-permute-start(bf16[16,2,64,128]{3,0,1,2:T(8,128)(2,1)} %get-tuple-element.336), channel_id=1, source_target_pairs={{0,1},{1,2},{2,3},{3,4},{4,5},{5,6},{6,7},{7,8},{8,9},{9,10},{10,1... | collective-permute-start | bytes 1572872 | tf_op jit(solution)/shard_map/ppermute | solution.py:41
  1184.9 2.8 copy-start.25
  (59 other events, 102.6 us)
Sparse Core Ops, SparseCore 0:
  55.8 266.6 all-reduce.14
  953.2 174.8 all-reduce.16
